TPU v7x, 32 devices: a whole 2x2x4 slice. The times are simulated.
32 devices in a mesh: row: 8 (over z, y), rep: 4 (over x, core).
Axes of the slice: x: 2, y: 2, z: 4, core: 2. Of those that a mesh axis runs over, the one named last changes fastest.
Arguments:
- features: bfloat16 [8192, 128], P(('row', 'rep')), may hold values from -0.0625 to 0.0625
- grad_out: bfloat16 [8192, 256], P(('row', 'rep')), may hold values from -6 to 6
- weight: bfloat16 [128, 256], replicated, may hold values from -0.375 to 0.375
- tile_vals: bfloat16 [8, 4, 8, 40, 128, 128], P('row', 'rep'), may hold values from -0.0625 to 0.0625
- tile_rows: int32 [8, 4, 8, 40], P('row', 'rep'), may hold values from 0 to 1
- tile_cols: int32 [8, 4, 8, 40], P('row', 'rep'), may hold values from 0 to 7
- tile_counts: int32 [8, 4, 8], P('row', 'rep'), may hold values from 10 to 40, as said below
Outputs:
- input_grad: bfloat16 [8192, 128], P(('row', 'rep'))
- weight_grad: float32 [128, 256], replicated
Inputs may be any that keep to these rules, and one draw needn't show every extreme that they name: Only the first tile_counts[b, c, s] slots of a device's offset s are live. In every draw one row block has all 40 slots live at every offset on every piece.
All inputs are finite; a program needn't handle non-finite values.
Results may differ from a plain program's by a relative error of at most 0.001.
Values may be sent and summed in bfloat16 or wider, within the bound.
A program may use at most 128 MiB of HBM per device.

v0:
```python
import functools

import jax
import jax.numpy as jnp
from jax import lax
from jax.experimental import pallas as pl
from jax.experimental.pallas import tpu as pltpu
from jax.sharding import PartitionSpec as P

MESH = pl.DeviceIdType.MESH
GROUP = 40


def in_hbm(value):
    return pltpu.with_memory_space_constraint(value, pltpu.HBM)


def gather_kernel(n_row, n_rep, offsets, chain, g_ref, f_ref, weight_in, vals_in, gall_ref, fall_ref, weight_ref, vals_ref, send_sem, recv_sem, fsend_sem, frecv_sem, local_sem, vals_sem):
    row, rep = lax.axis_index("row"), lax.axis_index("rep")
    barrier = pltpu.get_barrier_semaphore()
    loads = [
        pltpu.make_async_copy(g_ref, gall_ref.at[row], local_sem.at[0]),
        pltpu.make_async_copy(f_ref, fall_ref.at[rep], local_sem.at[1]),
        pltpu.make_async_copy(weight_in, weight_ref, local_sem.at[2]),
    ]
    for s in range(offsets):
        loads.append(pltpu.make_async_copy(vals_in.at[0, 0, s], vals_ref.at[s], vals_sem.at[s]))

    def piece_copy(way, origin, half, target, own):
        return pltpu.make_async_remote_copy(
            src_ref=g_ref.at[half] if own else gall_ref.at[origin, half],
            dst_ref=gall_ref.at[origin, half],
            send_sem=send_sem.at[way, origin, half],
            recv_sem=recv_sem.at[origin, half],
            device_id=(target, rep), device_id_type=MESH)

    for k in range(1, n_rep):
        pl.semaphore_signal(barrier, inc=1, device_id=(row, lax.rem(rep + k, n_rep)), device_id_type=MESH)
    if chain:
        z, y = row // 2, row % 2
        length = n_row // 2
        beside, above, below = row + 1 - 2 * y, row + 2, row - 2
        has_above, has_below = z < length - 1, z > 0
        pl.semaphore_signal(barrier, inc=1, device_id=(beside, rep), device_id_type=MESH)

        @pl.when(has_above)
        def _():
            pl.semaphore_signal(barrier, inc=1, device_id=(above, rep), device_id_type=MESH)

        @pl.when(has_below)
        def _():
            pl.semaphore_signal(barrier, inc=1, device_id=(below, rep), device_id_type=MESH)

        pl.semaphore_wait(barrier, n_rep + has_above.astype(jnp.int32) + has_below.astype(jnp.int32))
    else:
        shifts = sorted({k % n_row for k in range(1, offsets)} | {-k % n_row for k in range(1, offsets)})
        for k in shifts:
            pl.semaphore_signal(barrier, inc=1, device_id=(lax.rem(row + k, n_row), rep), device_id_type=MESH)
        pl.semaphore_wait(barrier, len(shifts) + n_rep - 1)

    feat_copies = []
    for k in range(1, n_rep):
        feat_copies.append(pltpu.make_async_remote_copy(
            src_ref=f_ref, dst_ref=fall_ref.at[rep], send_sem=fsend_sem.at[k], recv_sem=frecv_sem.at[k],
            device_id=(row, lax.rem(rep + k, n_rep)), device_id_type=MESH))

    def start_rest():
        for copy in feat_copies:
            copy.start()
        for load in loads:
            load.start()
        gall_ref[n_row] = jnp.zeros(gall_ref.shape[1:], gall_ref.dtype)

    if chain:
        def send(cond, way, origin, half, target, own=False):
            pl.when(cond)(piece_copy(way, origin, half, target, own).start)

        always = row >= 0
        send(always, 0, row, 0, beside, True)
        send(has_above, 1, row, 1, above, True)
        send(has_below, 2, row, 1, below, True)
        send(has_above, 1, row, 0, above, True)
        send(has_below, 2, row, 0, below, True)
        send(always, 0, row, 1, beside, True)
        start_rest()
        piece_copy(0, beside, 0, beside, False).wait_recv()
        send(has_above, 1, beside, 0, above)
        send(has_below, 2, beside, 0, below)
        for dist in range(1, length):
            for down in (False, True):
                far = z + dist if down else z - dist
                there = far < length if down else far >= 0
                mine, other = far * 2 + y, far * 2 + 1 - y
                way, onward, target = (2, has_below, below) if down else (1, has_above, above)

                @pl.when(there)
                def _():
                    piece_copy(0, mine, 1, beside, False).wait_recv()
                    send(onward, way, mine, 1, target)
                    send(always, 0, mine, 1, beside)
                    piece_copy(0, mine, 0, beside, False).wait_recv()
                    send(onward, way, mine, 0, target)
                    piece_copy(0, other, 0, beside, False).wait_recv()
                    send(onward, way, other, 0, target)

        piece_copy(0, beside, 1, beside, False).wait_recv()
        for dist in range(1, length):
            for down in (False, True):
                far = z + dist if down else z - dist
                there = far < length if down else far >= 0
                other = far * 2 + 1 - y

                @pl.when(there)
                def _():
                    piece_copy(0, other, 1, beside, False).wait_recv()

        for load in loads:
            load.wait()
        for copy in feat_copies:
            copy.wait()
        for dist in range(length):
            for down in (False, True) if dist else (False,):
                far = z + dist if down else z - dist
                there = far < length if down else far >= 0
                mine, other = far * 2 + y, far * 2 + 1 - y
                outs = []
                if dist == 0:
                    outs += [(always, 0, mine, 0), (always, 0, mine, 1)]
                    for origin, half in ((mine, 0), (mine, 1), (other, 0)):
                        outs += [(has_above, 1, origin, half), (has_below, 2, origin, half)]
                else:
                    way, onward = (2, has_below) if down else (1, has_above)
                    outs += [(always, 0, mine, 1)]
                    outs += [(onward, way, origin, half) for origin, half in ((mine, 1), (mine, 0), (other, 0))]
                for cond, way, origin, half in outs:
                    copy = piece_copy(way, origin, half, beside, False)
                    pl.when(jnp.logical_and(there, cond))(copy.wait_send)
    else:
        copies = []
        for k in range(1, offsets):
            copies.append(pltpu.make_async_remote_copy(
                src_ref=g_ref, dst_ref=gall_ref.at[row], send_sem=send_sem.at[0, k, 0], recv_sem=recv_sem.at[k, 0],
                device_id=(lax.rem(row + k, n_row), rep), device_id_type=MESH))
        for copy in copies:
            copy.start()
        start_rest()
        for load in loads:
            load.wait()
        for copy in feat_copies + copies:
            copy.wait()


def gather(grad_out, features, weight, tile_vals, n_row, n_rep):
    offsets, slots, tile = tile_vals.shape[2:5]
    rows_dev, hidden = grad_out.shape
    chain = n_row == offsets and n_row % 2 == 0 and n_row >= 4 and rows_dev == 2 * tile
    vmem = pl.BlockSpec(memory_space=pltpu.VMEM)
    dma = pltpu.SemaphoreType.DMA
    return pl.pallas_call(
        functools.partial(gather_kernel, n_row, n_rep, offsets, chain),
        out_shape=(
            jax.ShapeDtypeStruct((n_row + 1, rows_dev // tile, tile, hidden), grad_out.dtype),
            jax.ShapeDtypeStruct((n_rep,) + features.shape, features.dtype),
            jax.ShapeDtypeStruct(weight.shape, weight.dtype),
            jax.ShapeDtypeStruct(tile_vals.shape[2:], tile_vals.dtype),
        ),
        in_specs=[pl.BlockSpec(memory_space=pltpu.HBM)] * 4,
        out_specs=(vmem,) * 4,
        scratch_shapes=[
            dma((3, n_row, 2)),
            dma((n_row, 2)),
            dma((n_rep,)),
            dma((n_rep,)),
            dma((3,)),
            dma((offsets,)),
        ],
        compiler_params=pltpu.CompilerParams(collective_id=0, has_side_effects=True, vmem_limit_bytes=24 * 2**20),
        name="gather_sources",
    )(*map(in_hbm, (grad_out.reshape(rows_dev // tile, tile, hidden), features, weight, tile_vals)))


def dot_first(left, right):
    return lax.dot_general(left, right, (((0,), (0,)), ((), ())), preferred_element_type=jnp.float32)


def split(value):
    high = value.astype(jnp.bfloat16)
    low = (value - high.astype(jnp.float32)).astype(jnp.bfloat16)
    return high, low


def tiles_kernel(offsets, tile, col_tiles, rows_in, cols_in, counts_in, vals, blocks, fall_ref, weight_ref, ig_ref, wg_ref, totals, rows_ref, cols_ref, counts_ref, sem):
    loads = [
        pltpu.make_async_copy(rows_in, rows_ref, sem.at[0]),
        pltpu.make_async_copy(cols_in, cols_ref, sem.at[1]),
        pltpu.make_async_copy(counts_in, counts_ref, sem.at[2]),
    ]
    for load in loads:
        load.start()
    totals[...] = jnp.zeros_like(totals)
    row, n_row = lax.axis_index("row"), lax.axis_size("row")
    for load in loads:
        load.wait()

    def one_offset(s, carry):
        count = counts_ref[0, 0, s]
        origin = lax.rem(row + n_row - s, n_row)

        def one_group(group, carry):
            parts = []
            for u in range(GROUP):
                k = group * GROUP + u
                chosen = blocks[jnp.where(k < count, origin, n_row), rows_ref[0, 0, s, k]]
                parts.append((cols_ref[0, 0, s, k], dot_first(vals[s, k], chosen)))
            for col, part in parts:
                totals[col] += part
            return carry

        return lax.fori_loop(0, (count + GROUP - 1) // GROUP, one_group, carry)

    lax.fori_loop(0, offsets, one_offset, 0)
    weight = weight_ref[...]
    feats, hidden = weight.shape

    def one_col(col, wg):
        high, low = split(totals[col])
        dims = (((1,), (1,)), ((), ()))
        ig_ref[col] = (
            lax.dot_general(high, weight, dims, preferred_element_type=jnp.float32)
            + lax.dot_general(low, weight, dims, preferred_element_type=jnp.float32))
        return wg + dot_first(fall_ref[col], high) + dot_first(fall_ref[col], low)

    wg = jnp.zeros((feats, hidden), jnp.float32)
    if col_tiles <= 8:
        for col in range(col_tiles):
            wg = one_col(col, wg)
    else:
        wg = lax.fori_loop(0, col_tiles, one_col, wg)
    for chunk in range(wg_ref.shape[0]):
        i, j = chunk // (hidden // 128), chunk % (hidden // 128)
        wg_ref[chunk] = wg[8 * i:8 * i + 8, 128 * j:128 * j + 128]


def tile_products(tile_rows, tile_cols, tile_counts, vals, gall, fall, weight):
    offsets, slots, tile = vals.shape[:3]
    row_tiles, hidden = gall.shape[1], gall.shape[3]
    n_rep, _, feats = fall.shape
    col_tiles = n_rep * row_tiles
    vmem = pl.BlockSpec(memory_space=pltpu.VMEM)
    hbm = pl.BlockSpec(memory_space=pltpu.HBM)
    return pl.pallas_call(
        functools.partial(tiles_kernel, offsets, tile, col_tiles),
        out_shape=(
            jax.ShapeDtypeStruct((col_tiles, tile, feats), jnp.float32),
            jax.ShapeDtypeStruct((feats * hidden // 1024, 8, 128), jnp.float32),
        ),
        in_specs=[hbm, hbm, hbm, vmem, vmem, vmem, vmem],
        out_specs=(vmem, vmem),
        scratch_shapes=[
            pltpu.VMEM((col_tiles, tile, hidden), jnp.float32),
            pltpu.SMEM(tile_rows.shape, jnp.int32),
            pltpu.SMEM(tile_cols.shape, jnp.int32),
            pltpu.SMEM(tile_counts.shape, jnp.int32),
            pltpu.SemaphoreType.DMA((3,)),
        ],
        compiler_params=pltpu.CompilerParams(vmem_limit_bytes=32 * 2**20),
        name="tile_products",
    )(in_hbm(tile_rows), in_hbm(tile_cols), in_hbm(tile_counts), vals, gall, fall.reshape(col_tiles, tile, feats), weight)


def reduce_kernel(n_row, n_rep, ig_ref, wg_ref, out_ref, wout_ref, pair_buf, mid_buf, ig_buf, wg_buf, row_buf, sum_buf, full_buf, pair_send, pair_recv, ig_send, ig_recv, wg_send, wg_recv, row_send, row_recv, sum_send, sum_recv, full_send, full_recv):
    row, rep = lax.axis_index("row"), lax.axis_index("rep")
    pairs = n_rep // 2
    pair, core = rep // 2, rep % 2
    chunks = wg_ref.shape[1]
    scatter = chunks % n_row == 0
    share = chunks // n_row if scatter else chunks
    barrier = pltpu.get_barrier_semaphore()
    for k in range(1, n_row):
        pl.semaphore_signal(barrier, inc=1, device_id=(lax.rem(row + k, n_row), rep), device_id_type=MESH)
    for k in range(1, n_rep):
        pl.semaphore_signal(barrier, inc=1, device_id=(row, lax.rem(rep + k, n_rep)), device_id_type=MESH)
    pl.semaphore_wait(barrier, n_row + n_rep - 2)

    started = []

    def copy_to(src, dst, send, recv, target):
        copy = pltpu.make_async_remote_copy(
            src_ref=src, dst_ref=dst, send_sem=send, recv_sem=recv, device_id=target, device_id_type=MESH)
        copy.start()
        started.append(copy)
        return copy

    wg_copies, pair_copies, ig_copies, row_copies, sum_copies, full_copies = [], [], [], [], [], []
    for k in range(1, n_rep):
        other = lax.rem(rep + k, n_rep)
        wg_copies.append(copy_to(wg_ref.at[other], wg_buf.at[rep], wg_send.at[k], wg_recv.at[k], (row, other)))
    for k in range(1, pairs + 1):
        block = lax.rem(pair + k, pairs)
        pair_copies.append(copy_to(
            ig_ref.at[block * 2 + 1 - core], pair_buf.at[block], pair_send.at[k - 1], pair_recv.at[k - 1],
            (row, rep + 1 - 2 * core)))
    for k in range(1, pairs):
        block = lax.rem(pair + k, pairs)
        pair_copies[k - 1].wait_recv()
        mid_buf[block] = ig_ref[block * 2 + core] + pair_buf[block]
        ig_copies.append(copy_to(
            mid_buf.at[block], ig_buf.at[pair], ig_send.at[k], ig_recv.at[k], (row, block * 2 + core)))
    wg_buf[rep] = wg_ref[rep]
    for copy in wg_copies:
        copy.wait_recv()
    total = wg_buf[0]
    for k in range(1, n_rep):
        total = total + wg_buf[k]
    sum_buf[...] = total.reshape(sum_buf.shape)
    for k in range(1, n_row):
        other = lax.rem(row + k, n_row)
        source = sum_buf.at[other] if scatter else sum_buf.at[0]
        row_copies.append(copy_to(source, row_buf.at[row], row_send.at[k], row_recv.at[k], (other, rep)))
    row_buf[row] = sum_buf[row] if scatter else sum_buf[0]
    for copy in row_copies:
        copy.wait_recv()
    total = row_buf[0]
    for k in range(1, n_row):
        total = total + row_buf[k]
    if scatter:
        full_buf[rep, row] = total
        for k in range(1, n_row):
            other = lax.rem(row + k, n_row)
            sum_copies.append(copy_to(
                full_buf.at[rep, row], full_buf.at[rep, row], sum_send.at[k], sum_recv.at[k], (other, rep)))
        for copy in sum_copies:
            copy.wait_recv()
    else:
        full_buf[rep, 0] = total
    for k in range(1, n_rep):
        other = lax.rem(rep + k, n_rep)
        full_copies.append(copy_to(
            full_buf.at[rep], full_buf.at[rep], full_send.at[k], full_recv.at[k], (row, other)))
    pair_copies[pairs - 1].wait_recv()
    total = ig_ref[rep] + pair_buf[pair]
    for k in range(1, pairs):
        ig_copies[k - 1].wait_recv()
        total = total + ig_buf[lax.rem(pair - k + pairs, pairs)]
    out_ref[...] = total.astype(out_ref.dtype)
    for copy in full_copies:
        copy.wait_recv()
    across = wout_ref.shape[1] // 128
    full = full_buf[...].reshape((n_rep * chunks, 8, 128))
    for chunk in range(n_rep * chunks):
        i, j = chunk // across, chunk % across
        wout_ref[8 * i:8 * i + 8, 128 * j:128 * j + 128] = full[chunk]
    for copy in started:
        copy.wait_send()


def reduce(ig_part, wg_part, feats, hidden, n_row, n_rep):
    chunks = wg_part.shape[0] // n_rep
    scatter = chunks % n_row == 0
    owners = n_row if scatter else 1
    share = chunks // owners
    rows_dev = ig_part.shape[0] * ig_part.shape[1] // n_rep
    width = ig_part.shape[2]
    pairs = n_rep // 2
    vmem = pl.BlockSpec(memory_space=pltpu.VMEM)
    dma = pltpu.SemaphoreType.DMA
    return pl.pallas_call(
        functools.partial(reduce_kernel, n_row, n_rep),
        out_shape=(
            jax.ShapeDtypeStruct((rows_dev, width), jnp.bfloat16),
            jax.ShapeDtypeStruct((feats, hidden), jnp.float32),
        ),
        in_specs=[vmem, vmem],
        out_specs=(vmem, vmem),
        scratch_shapes=[
            pltpu.VMEM((pairs, rows_dev, width), jnp.float32),
            pltpu.VMEM((pairs, rows_dev, width), jnp.float32),
            pltpu.VMEM((pairs, rows_dev, width), jnp.float32),
            pltpu.VMEM((n_rep, chunks, 8, 128), jnp.float32),
            pltpu.VMEM((n_row, share, 8, 128), jnp.float32),
            pltpu.VMEM((owners, share, 8, 128), jnp.float32),
            pltpu.VMEM((n_rep, owners, share, 8, 128), jnp.float32),
            dma((pairs,)), dma((pairs,)), dma((pairs,)), dma((pairs,)),
            dma((n_rep,)), dma((n_rep,)), dma((n_row,)), dma((n_row,)),
            dma((n_row,)), dma((n_row,)), dma((n_rep,)), dma((n_rep,)),
        ],
        compiler_params=pltpu.CompilerParams(collective_id=1, has_side_effects=True, vmem_limit_bytes=32 * 2**20),
        name="reduce_grads",
    )(ig_part.reshape(n_rep, rows_dev, width), wg_part.reshape(n_rep, chunks, 8, 128))


def on_device(features, grad_out, weight, tile_vals, tile_rows, tile_cols, tile_counts):
    n_row, n_rep = lax.axis_size("row"), lax.axis_size("rep")
    gall, fall, weight_near, vals = gather(grad_out, features, weight, tile_vals, n_row, n_rep)
    ig_part, wg_part = tile_products(tile_rows, tile_cols, tile_counts, vals, gall, fall, weight_near)
    return reduce(ig_part, wg_part, weight.shape[0], weight.shape[1], n_row, n_rep)


def solution(mesh):
    placed = (
        P(("row", "rep"), None),
        P(("row", "rep"), None),
        P(),
        P("row", "rep", None, None, None, None),
        P("row", "rep", None, None),
        P("row", "rep", None, None),
        P("row", "rep", None),
    )
    return jax.shard_map(
        on_device,
        mesh=mesh,
        in_specs=placed,
        out_specs=(P(("row", "rep"), None), P()),
        check_vma=False,
    )
```

profile of v0, /device:TPU:0, one launch (start us, length us, event | category | flops | bytes accessed | tf_op | source)
XLA Modules:
  0.0 49.7 jit_solution(10485619342709468954)
XLA Ops:
  0.6 22.3 %gather_sources.1 = (bf16[9,2,128,256]{3,2,1,0:T(8,128)(2,1)S(1)}, bf16[4,256,128]{2,1,0:T(8,128)(2,1)S(1)}, bf16[128,256]{1,0:T(8,128)(2,1)S(1)}, bf16[8,40,128,128]{3,2,1,0:T(8,128)(2,1)S(1)}) custom-call(bf16[2,128,256]{2,1,0:T(8,128)(2,1)} %bitcast.7, bf16[256,128]{1,0:T(8,128)(2,1)} %f_ref.1, bf16[128,256]{1,0:T(8,128)(2,1)} %weight_in.1, ...), custom_call_target="tpu_custom_call" | custom-call | tf_op jit(solution)/shard_map/gather_sources/pallas_call | solution.py:159
  23.0 8.8 %tile_products.1 = (f32[8,128,128]{2,1,0:T(8,128)S(1)}, f32[32,8,128]{2,1,0:T(8,128)S(1)}) custom-call(s32[1,1,8,40]{3,2,1,0:T(8,128)} %rows_in.1, s32[1,1,8,40]{3,2,1,0:T(8,128)} %cols_in.1, s32[1,1,8]{2,1,0:T(1,128)} %counts_in.1, bf16[8,40,128,128]{3,2,1,0:T(8,128)(2,1)S(1)} %get-tuple-element.8.vals, ...), custom_call_target="tpu_custom_call" | custom-call | tf_op jit(solution)/shard_map/tile_products/pallas_call | solution.py:251
  31.8 16.6 %reduce_grads.1 = (bf16[256,128]{1,0:T(8,128)(2,1)S(1)}, f32[128,256]{1,0:T(8,128)S(1)}) custom-call(f32[4,256,128]{2,1,0:T(8,128)S(1)} %bitcast.4, f32[4,8,8,128]{3,2,1,0:T(8,128)S(1)} %bitcast.6), custom_call_target="tpu_custom_call" | custom-call | tf_op jit(solution)/shard_map/reduce_grads/pallas_call | solution.py:367
  48.4 0.6 %copy.11 = bf16[256,128]{1,0:T(8,128)(2,1)} copy(bf16[256,128]{1,0:T(8,128)(2,1)S(1)} %get-tuple-element.16) | data formatting | bytes 131072
  49.0 0.7 %copy.12 = f32[128,256]{1,0:T(8,128)} copy(f32[128,256]{1,0:T(8,128)S(1)} %get-tuple-element.17) | data formatting | bytes 262144
where the time goes:
time: 49.9 us; the launch traced here: 49.7 us
  Pallas kernels  47.8 us (96%)
  local copies, waits for them, and re-layouts  1.29 us (3%)
  between operations  0.66 us (1%)
    pallas_call x1, Pallas kernels, gather(): pl.pallas_call(functools.partial(gather_kernel, n_row, n_rep, offsets, ch...  22.3 us
    pallas_call x1, Pallas kernels, reduce(): pl.pallas_call(functools.partial(reduce_kernel, n_row, n_rep), out_shape=...  16.6 us
    pallas_call x1, Pallas kernels, tile_products(): pl.pallas_call(functools.partial(tiles_kernel, offsets, tile, col_tiles),...  8.81 us
    unnamed x2, local copies, waits for them, and re-layouts  1.29 us

commit v1 on v0

--- a/solution.py
+++ b/solution.py
@@ -26,6 +26,9 @@
     for s in range(offsets):
         loads.append(pltpu.make_async_copy(vals_in.at[0, 0, s], vals_ref.at[s], vals_sem.at[s]))
 
+    for load in loads:
+        load.start()
+
     def piece_copy(way, origin, half, target, own):
         return pltpu.make_async_remote_copy(
             src_ref=g_ref.at[half] if own else gall_ref.at[origin, half],
@@ -67,8 +70,6 @@
     def start_rest():
         for copy in feat_copies:
             copy.start()
-        for load in loads:
-            load.start()
         gall_ref[n_row] = jnp.zeros(gall_ref.shape[1:], gall_ref.dtype)
 
     if chain:
@@ -87,21 +88,20 @@
         send(has_above, 1, beside, 0, above)
         send(has_below, 2, beside, 0, below)
         for dist in range(1, length):
-            for down in (False, True):
-                far = z + dist if down else z - dist
-                there = far < length if down else far >= 0
-                mine, other = far * 2 + y, far * 2 + 1 - y
-                way, onward, target = (2, has_below, below) if down else (1, has_above, above)
-
-                @pl.when(there)
-                def _():
-                    piece_copy(0, mine, 1, beside, False).wait_recv()
-                    send(onward, way, mine, 1, target)
-                    send(always, 0, mine, 1, beside)
-                    piece_copy(0, mine, 0, beside, False).wait_recv()
-                    send(onward, way, mine, 0, target)
-                    piece_copy(0, other, 0, beside, False).wait_recv()
-                    send(onward, way, other, 0, target)
+            for item in range(3):
+                for down in (False, True):
+                    far = z + dist if down else z - dist
+                    there = far < length if down else far >= 0
+                    origin = far * 2 + (1 - y if item == 2 else y)
+                    half = 1 if item == 0 else 0
+                    way, onward, target = (2, has_below, below) if down else (1, has_above, above)
+
+                    @pl.when(there)
+                    def _():
+                        piece_copy(0, origin, half, beside, False).wait_recv()
+                        send(onward, way, origin, half, target)
+                        if item == 0:
+                            send(always, 0, origin, half, beside)
 
         piece_copy(0, beside, 1, beside, False).wait_recv()
         for dist in range(1, length):
@@ -268,7 +268,7 @@
     )(in_hbm(tile_rows), in_hbm(tile_cols), in_hbm(tile_counts), vals, gall, fall.reshape(col_tiles, tile, feats), weight)
 
 
-def reduce_kernel(n_row, n_rep, ig_ref, wg_ref, out_ref, wout_ref, pair_buf, mid_buf, ig_buf, wg_buf, row_buf, sum_buf, full_buf, pair_send, pair_recv, ig_send, ig_recv, wg_send, wg_recv, row_send, row_recv, sum_send, sum_recv, full_send, full_recv):
+def reduce_kernel(n_row, n_rep, ig_ref, wg_ref, out_ref, wout_ref, pair_buf, mid_buf, ig_buf, wg_buf, row_buf, sum_buf, full_buf, pair_send, pair_recv, ig_send, ig_recv, wg_send, wg_recv, row_send, row_recv, full_send, full_recv):
     row, rep = lax.axis_index("row"), lax.axis_index("rep")
     pairs = n_rep // 2
     pair, core = rep // 2, rep % 2
@@ -276,11 +276,11 @@
     scatter = chunks % n_row == 0
     share = chunks // n_row if scatter else chunks
     barrier = pltpu.get_barrier_semaphore()
-    for k in range(1, n_row):
-        pl.semaphore_signal(barrier, inc=1, device_id=(lax.rem(row + k, n_row), rep), device_id_type=MESH)
-    for k in range(1, n_rep):
-        pl.semaphore_signal(barrier, inc=1, device_id=(row, lax.rem(rep + k, n_rep)), device_id_type=MESH)
-    pl.semaphore_wait(barrier, n_row + n_rep - 2)
+    peers = [(i, j) for i in range(n_row) for j in range(n_rep) if (i or j) and (scatter or not (i and j))]
+    for i, j in peers:
+        pl.semaphore_signal(
+            barrier, inc=1, device_id=(lax.rem(row + i, n_row), lax.rem(rep + j, n_rep)), device_id_type=MESH)
+    pl.semaphore_wait(barrier, len(peers))
 
     started = []
 
@@ -291,7 +291,7 @@
         started.append(copy)
         return copy
 
-    wg_copies, pair_copies, ig_copies, row_copies, sum_copies, full_copies = [], [], [], [], [], []
+    wg_copies, pair_copies, ig_copies, row_copies, full_copies = [], [], [], [], []
     for k in range(1, n_rep):
         other = lax.rem(rep + k, n_rep)
         wg_copies.append(copy_to(wg_ref.at[other], wg_buf.at[rep], wg_send.at[k], wg_recv.at[k], (row, other)))
@@ -325,18 +325,16 @@
         total = total + row_buf[k]
     if scatter:
         full_buf[rep, row] = total
-        for k in range(1, n_row):
-            other = lax.rem(row + k, n_row)
-            sum_copies.append(copy_to(
-                full_buf.at[rep, row], full_buf.at[rep, row], sum_send.at[k], sum_recv.at[k], (other, rep)))
-        for copy in sum_copies:
-            copy.wait_recv()
+        for i, j in peers:
+            full_copies.append(copy_to(
+                full_buf.at[rep, row], full_buf.at[rep, row], full_send.at[i, j], full_recv.at[i, j],
+                (lax.rem(row + i, n_row), lax.rem(rep + j, n_rep))))
     else:
         full_buf[rep, 0] = total
-    for k in range(1, n_rep):
-        other = lax.rem(rep + k, n_rep)
-        full_copies.append(copy_to(
-            full_buf.at[rep], full_buf.at[rep], full_send.at[k], full_recv.at[k], (row, other)))
+        for k in range(1, n_rep):
+            other = lax.rem(rep + k, n_rep)
+            full_copies.append(copy_to(
+                full_buf.at[rep], full_buf.at[rep], full_send.at[0, k], full_recv.at[0, k], (row, other)))
     pair_copies[pairs - 1].wait_recv()
     total = ig_ref[rep] + pair_buf[pair]
     for k in range(1, pairs):
@@ -382,7 +380,7 @@
             pltpu.VMEM((n_rep, owners, share, 8, 128), jnp.float32),
             dma((pairs,)), dma((pairs,)), dma((pairs,)), dma((pairs,)),
             dma((n_rep,)), dma((n_rep,)), dma((n_row,)), dma((n_row,)),
-            dma((n_row,)), dma((n_row,)), dma((n_rep,)), dma((n_rep,)),
+            dma((n_row, n_rep)), dma((n_row, n_rep)),
         ],
         compiler_params=pltpu.CompilerParams(collective_id=1, has_side_effects=True, vmem_limit_bytes=32 * 2**20),
         name="reduce_grads",

time: 49.9 us -> 48.6 us (0.974)
  Pallas kernels: 47.8 us -> 46.5 us
    pallas_call x1, Pallas kernels: 22.3 us -> 21.3 us  [gather(): pl.pallas_call(functools.partial(gather_kernel, n_row, n_rep, offsets, ch...]
where the time goes in v1:
time: 48.6 us; the launch traced here: 48.4 us
  Pallas kernels  46.5 us (96%)
  local copies, waits for them, and re-layouts  1.29 us (3%)
  between operations  0.66 us (1%)
    pallas_call x1, Pallas kernels, gather(): pl.pallas_call(functools.partial(gather_kernel, n_row, n_rep, offsets, ch...  21.3 us
    pallas_call x1, Pallas kernels, reduce(): pl.pallas_call(functools.partial(reduce_kernel, n_row, n_rep), out_shape=...  16.4 us
    pallas_call x1, Pallas kernels, tile_products(): pl.pallas_call(functools.partial(tiles_kernel, offsets, tile, col_tiles),...  8.81 us
    unnamed x2, local copies, waits for them, and re-layouts  1.29 us

profile of v1, /device:TPU:0, one launch (start us, length us, event | category | flops | bytes accessed | tf_op | source)
XLA Modules:
  0.0 48.4 jit_solution(799188455921321983)
XLA Ops:
  0.6 21.3 %gather_sources.1 = (bf16[9,2,128,256]{3,2,1,0:T(8,128)(2,1)S(1)}, bf16[4,256,128]{2,1,0:T(8,128)(2,1)S(1)}, bf16[128,256]{1,0:T(8,128)(2,1)S(1)}, bf16[8,40,128,128]{3,2,1,0:T(8,128)(2,1)S(1)}) custom-call(bf16[2,128,256]{2,1,0:T(8,128)(2,1)} %bitcast.7, bf16[256,128]{1,0:T(8,128)(2,1)} %f_ref.1, bf16[128,256]{1,0:T(8,128)(2,1)} %weight_in.1, ...), custom_call_target="tpu_custom_call" | custom-call | tf_op jit(solution)/shard_map/gather_sources/pallas_call | solution.py:159
  21.9 8.8 %tile_products.1 = (f32[8,128,128]{2,1,0:T(8,128)S(1)}, f32[32,8,128]{2,1,0:T(8,128)S(1)}) custom-call(s32[1,1,8,40]{3,2,1,0:T(8,128)} %rows_in.1, s32[1,1,8,40]{3,2,1,0:T(8,128)} %cols_in.1, s32[1,1,8]{2,1,0:T(1,128)} %counts_in.1, bf16[8,40,128,128]{3,2,1,0:T(8,128)(2,1)S(1)} %get-tuple-element.8.vals, ...), custom_call_target="tpu_custom_call" | custom-call | tf_op jit(solution)/shard_map/tile_products/pallas_call | solution.py:251
  30.7 16.4 %reduce_grads.1 = (bf16[256,128]{1,0:T(8,128)(2,1)S(1)}, f32[128,256]{1,0:T(8,128)S(1)}) custom-call(f32[4,256,128]{2,1,0:T(8,128)S(1)} %bitcast.4, f32[4,8,8,128]{3,2,1,0:T(8,128)S(1)} %bitcast.6), custom_call_target="tpu_custom_call" | custom-call | tf_op jit(solution)/shard_map/reduce_grads/pallas_call | solution.py:365
  47.1 0.6 %copy.11 = bf16[256,128]{1,0:T(8,128)(2,1)} copy(bf16[256,128]{1,0:T(8,128)(2,1)S(1)} %get-tuple-element.16) | data formatting | bytes 131072
  47.8 0.7 %copy.12 = f32[128,256]{1,0:T(8,128)} copy(f32[128,256]{1,0:T(8,128)S(1)} %get-tuple-element.17) | data formatting | bytes 262144

commit v2 on v1

--- a/solution.py
+++ b/solution.py
@@ -268,7 +268,7 @@
     )(in_hbm(tile_rows), in_hbm(tile_cols), in_hbm(tile_counts), vals, gall, fall.reshape(col_tiles, tile, feats), weight)
 
 
-def reduce_kernel(n_row, n_rep, ig_ref, wg_ref, out_ref, wout_ref, pair_buf, mid_buf, ig_buf, wg_buf, row_buf, sum_buf, full_buf, pair_send, pair_recv, ig_send, ig_recv, wg_send, wg_recv, row_send, row_recv, full_send, full_recv):
+def reduce_kernel(n_row, n_rep, ig_ref, wg_ref, out_ref, wout_ref, pair_buf, mid_buf, ig_buf, wg_buf, row_buf, sum_buf, full_buf, pair_send, pair_recv, ig_send, ig_recv, wg_send, wg_recv, row_send, row_recv, full_send, full_recv, all_buf, all_send, all_recv):
     row, rep = lax.axis_index("row"), lax.axis_index("rep")
     pairs = n_rep // 2
     pair, core = rep // 2, rep % 2
@@ -292,7 +292,12 @@
         return copy
 
     wg_copies, pair_copies, ig_copies, row_copies, full_copies = [], [], [], [], []
-    for k in range(1, n_rep):
+    for i, j in peers if scatter else ():
+        to_row, to_rep = lax.rem(row + i, n_row), lax.rem(rep + j, n_rep)
+        row_copies.append(copy_to(
+            wg_ref.at[to_rep, pl.ds(to_row * share, share)], all_buf.at[row, rep], all_send.at[i, j], all_recv.at[i, j],
+            (to_row, to_rep)))
+    for k in range(1, 1 if scatter else n_rep):
         other = lax.rem(rep + k, n_rep)
         wg_copies.append(copy_to(wg_ref.at[other], wg_buf.at[rep], wg_send.at[k], wg_recv.at[k], (row, other)))
     for k in range(1, pairs + 1):
@@ -306,23 +311,29 @@
         mid_buf[block] = ig_ref[block * 2 + core] + pair_buf[block]
         ig_copies.append(copy_to(
             mid_buf.at[block], ig_buf.at[pair], ig_send.at[k], ig_recv.at[k], (row, block * 2 + core)))
-    wg_buf[rep] = wg_ref[rep]
-    for copy in wg_copies:
-        copy.wait_recv()
-    total = wg_buf[0]
-    for k in range(1, n_rep):
-        total = total + wg_buf[k]
-    sum_buf[...] = total.reshape(sum_buf.shape)
-    for k in range(1, n_row):
-        other = lax.rem(row + k, n_row)
-        source = sum_buf.at[other] if scatter else sum_buf.at[0]
-        row_copies.append(copy_to(source, row_buf.at[row], row_send.at[k], row_recv.at[k], (other, rep)))
-    row_buf[row] = sum_buf[row] if scatter else sum_buf[0]
-    for copy in row_copies:
-        copy.wait_recv()
-    total = row_buf[0]
-    for k in range(1, n_row):
-        total = total + row_buf[k]
+    if scatter:
+        all_buf[row, rep] = wg_ref[rep, pl.ds(row * share, share)]
+        for copy in row_copies:
+            copy.wait_recv()
+        total = jnp.sum(all_buf[...], axis=(0, 1))
+    else:
+        wg_buf[rep] = wg_ref[rep]
+        for copy in wg_copies:
+            copy.wait_recv()
+        total = wg_buf[0]
+        for k in range(1, n_rep):
+            total = total + wg_buf[k]
+        sum_buf[...] = total.reshape(sum_buf.shape)
+        for k in range(1, n_row):
+            other = lax.rem(row + k, n_row)
+            source = sum_buf.at[0]
+            row_copies.append(copy_to(source, row_buf.at[row], row_send.at[k], row_recv.at[k], (other, rep)))
+        row_buf[row] = sum_buf[0]
+        for copy in row_copies:
+            copy.wait_recv()
+        total = row_buf[0]
+        for k in range(1, n_row):
+            total = total + row_buf[k]
     if scatter:
         full_buf[rep, row] = total
         for i, j in peers:
@@ -381,6 +392,8 @@
             dma((pairs,)), dma((pairs,)), dma((pairs,)), dma((pairs,)),
             dma((n_rep,)), dma((n_rep,)), dma((n_row,)), dma((n_row,)),
             dma((n_row, n_rep)), dma((n_row, n_rep)),
+            pltpu.VMEM((n_row, n_rep, share, 8, 128), jnp.float32),
+            dma((n_row, n_rep)), dma((n_row, n_rep)),
         ],
         compiler_params=pltpu.CompilerParams(collective_id=1, has_side_effects=True, vmem_limit_bytes=32 * 2**20),
         name="reduce_grads",

time: 48.6 us -> 47.9 us (0.986)
  Pallas kernels: 46.5 us -> 45.8 us
    pallas_call x1, Pallas kernels: 16.4 us -> 15.7 us  [reduce(): pl.pallas_call(functools.partial(reduce_kernel, n_row, n_rep), out_shape=...]
where the time goes in v2:
time: 47.9 us; the launch traced here: 47.7 us
  Pallas kernels  45.8 us (96%)
  local copies, waits for them, and re-layouts  1.29 us (3%)
  between operations  0.66 us (1%)
    pallas_call x1, Pallas kernels, gather(): pl.pallas_call(functools.partial(gather_kernel, n_row, n_rep, offsets, ch...  21.3 us
    pallas_call x1, Pallas kernels, reduce(): pl.pallas_call(functools.partial(reduce_kernel, n_row, n_rep), out_shape=...  15.7 us
    pallas_call x1, Pallas kernels, tile_products(): pl.pallas_call(functools.partial(tiles_kernel, offsets, tile, col_tiles),...  8.81 us
    unnamed x2, local copies, waits for them, and re-layouts  1.29 us

profile of v2, /device:TPU:0, one launch (start us, length us, event | category | flops | bytes accessed | tf_op | source)
XLA Modules:
  0.0 47.7 jit_solution(16974817368460663998)
XLA Ops:
  0.6 21.3 %gather_sources.1 = (bf16[9,2,128,256]{3,2,1,0:T(8,128)(2,1)S(1)}, bf16[4,256,128]{2,1,0:T(8,128)(2,1)S(1)}, bf16[128,256]{1,0:T(8,128)(2,1)S(1)}, bf16[8,40,128,128]{3,2,1,0:T(8,128)(2,1)S(1)}) custom-call(bf16[2,128,256]{2,1,0:T(8,128)(2,1)} %bitcast.7, bf16[256,128]{1,0:T(8,128)(2,1)} %f_ref.1, bf16[128,256]{1,0:T(8,128)(2,1)} %weight_in.1, ...), custom_call_target="tpu_custom_call" | custom-call | tf_op jit(solution)/shard_map/gather_sources/pallas_call | solution.py:159
  21.9 8.8 %tile_products.1 = (f32[8,128,128]{2,1,0:T(8,128)S(1)}, f32[32,8,128]{2,1,0:T(8,128)S(1)}) custom-call(s32[1,1,8,40]{3,2,1,0:T(8,128)} %rows_in.1, s32[1,1,8,40]{3,2,1,0:T(8,128)} %cols_in.1, s32[1,1,8]{2,1,0:T(1,128)} %counts_in.1, bf16[8,40,128,128]{3,2,1,0:T(8,128)(2,1)S(1)} %get-tuple-element.8.vals, ...), custom_call_target="tpu_custom_call" | custom-call | tf_op jit(solution)/shard_map/tile_products/pallas_call | solution.py:251
  30.7 15.7 %reduce_grads.1 = (bf16[256,128]{1,0:T(8,128)(2,1)S(1)}, f32[128,256]{1,0:T(8,128)S(1)}) custom-call(f32[4,256,128]{2,1,0:T(8,128)S(1)} %bitcast.4, f32[4,8,8,128]{3,2,1,0:T(8,128)S(1)} %bitcast.6), custom_call_target="tpu_custom_call" | custom-call | tf_op jit(solution)/shard_map/reduce_grads/pallas_call | solution.py:376
  46.5 0.6 %copy.11 = bf16[256,128]{1,0:T(8,128)(2,1)} copy(bf16[256,128]{1,0:T(8,128)(2,1)S(1)} %get-tuple-element.16) | data formatting | bytes 131072
  47.1 0.7 %copy.12 = f32[128,256]{1,0:T(8,128)} copy(f32[128,256]{1,0:T(8,128)S(1)} %get-tuple-element.17) | data formatting | bytes 262144
